TPU v7x, 128 devices: a whole 4x4x4 slice. The times are simulated.
128 devices in a mesh: section: 16 (over z, x), bond: 8 (over y, core).
Axes of the slice: x: 4, y: 4, z: 4, core: 2. Of those that a mesh axis runs over, the one named last changes fastest.
Arguments:
- site_tensor: float32 [16, 3072, 4, 3072], P('section', None, None, 'bond'), may hold values from -0.109375 to 0.109375
- boundary: float32 [128, 3072], replicated, may hold values from -6 to 6
- selected: int32 [16, 128], P('section'), may hold values from 0 to 3
Outputs:
- chosen_prob: float32 [16, 128], P('section')
- exit_rows: float32 [16, 128, 3072], P('section', None, 'bond')
All inputs are finite; a program needn't handle non-finite values.
Results may differ from a plain program's by a relative error of at most 0.0003.
Values sent between devices are 32-bit elements; how exact they have to be, the bound alone decides.
A program may use at most 128 MiB of HBM per device.

v0:
```python
import jax
import jax.numpy as jnp
from jax import lax
from jax.sharding import PartitionSpec as P

BATCH = 64


def from_behind(array, axis, by):
    count = lax.axis_size(axis)
    pairs = [(i, i + by) for i in range(count) if 0 <= i + by < count]
    return lax.ppermute(array, axis, pairs)


def finish(amplitudes, chosen, block_rows, outcomes, columns, width):
    shaped = amplitudes.reshape(block_rows, outcomes, columns)
    partial_weight = jnp.sum(shaped * shaped, axis=2)
    weight = lax.psum(partial_weight, "bond")
    outcome_ids = jnp.arange(outcomes, dtype=jnp.int32)
    onehot = (chosen[:, None] == outcome_ids[None, :]).astype(jnp.float32)
    chosen_weight = jnp.sum(onehot * weight, axis=1)
    prob_block = chosen_weight / jnp.sum(weight, axis=1)
    chosen_row = jnp.sum(onehot[:, :, None] * shaped, axis=1)
    next_block = chosen_row / jnp.sqrt(chosen_weight / width + 1e-06)[:, None]
    return (prob_block, next_block)


def on_device(site_tensor, boundary, selected):
    width = site_tensor.shape[1]
    outcomes = site_tensor.shape[2]
    columns = site_tensor.shape[3]
    site_matrix = site_tensor[0].reshape(width, outcomes * columns)
    sections = lax.axis_size("section")
    section_index = lax.axis_index("section")
    total_rows = boundary.shape[0]
    block_rows = BATCH
    micro_count = total_rows // block_rows
    picks = selected[0]
    start_rows = jnp.zeros((block_rows, width), jnp.float32)
    prob_init = jnp.zeros((total_rows,), jnp.float32)
    rows_init = jnp.zeros((total_rows, columns), jnp.float32)

    def advance(step_index, carry):
        incoming, prob_out, rows_out = carry
        micro = step_index - section_index
        valid = jnp.logical_and(micro >= 0, micro < micro_count)
        slot = jnp.clip(micro, 0, micro_count - 1)
        feed = jnp.clip(step_index, 0, micro_count - 1).astype(jnp.int32)
        fresh = lax.dynamic_slice_in_dim(boundary, feed * block_rows, block_rows, 0)
        chosen = lax.dynamic_slice_in_dim(picks, slot * block_rows, block_rows, 0)
        current = jnp.where(section_index == 0, fresh, incoming)
        amplitudes = jnp.dot(
            current,
            site_matrix,
            precision=lax.Precision.HIGHEST,
            preferred_element_type=jnp.float32,
        )
        prob_block, next_block = finish(amplitudes, chosen, block_rows, outcomes, columns, width)
        old_prob = lax.dynamic_slice_in_dim(prob_out, slot * block_rows, block_rows, 0)
        old_rows = lax.dynamic_slice_in_dim(rows_out, slot * block_rows, block_rows, 0)
        prob_out = lax.dynamic_update_slice_in_dim(
            prob_out, jnp.where(valid, prob_block, old_prob), slot * block_rows, 0
        )
        rows_out = lax.dynamic_update_slice_in_dim(
            rows_out, jnp.where(valid, next_block, old_rows), slot * block_rows, 0
        )
        whole_rows = lax.all_gather(next_block, "bond", axis=1, tiled=True)
        incoming = from_behind(whole_rows, "section", 1)
        return (incoming, prob_out, rows_out)

    final_carry = lax.fori_loop(
        0, micro_count + sections - 1, advance, (start_rows, prob_init, rows_init)
    )
    return (final_carry[1][None, :], final_carry[2][None, :, :])


def solution(mesh):
    in_specs = (P("section", None, None, "bond"), P(), P("section", None))
    out_specs = (P("section", None), P("section", None, "bond"))
    return jax.shard_map(
        on_device, mesh=mesh, in_specs=in_specs, out_specs=out_specs, check_vma=False
    )
```

profile of v0, /device:TPU:96, one launch (start us, length us, event | category | flops | bytes accessed | tf_op | source)
XLA Modules:
  0.0 1322.7 jit_solution(2115595274633260697)
XLA Ops:
  0.7 16.5 %copy.5 = f32[384,8,4,384]{3,1,2,0:T(8,128)} copy(f32[384,8,4,384]{3,2,1,0:T(4,128)} %bitcast.10) | data formatting | bytes 37748736
  17.3 1304.8 %while.18 = (s32[]{:T(128)}, f32[64,3072]{1,0:T(8,128)S(1)}, f32[128]{0:T(128)S(1)}, f32[128,384]{1,0:T(8,128)S(1)}, s32[]{:T(128)}, /*index=5*/s32[128]{0:T(128...) while((s32[]{:T(128)}, f32[64,3072]{1,0:T(8,128)S(1)}, ...), condition=%wide.region_6.7_spmd, body=%wide.region_0.6_spmd.sunk | while | flops 3624494848 | bytes 26552424 | solution.py:71
  32.7 25.9 %psum.13 = f32[64,4]{1,0:T(8,128)S(1)} all-reduce(f32[64,4]{1,0:T(8,128)S(1)} %get-tuple-element.271), channel_id=1, replica_groups=mesh['section'=16,'bond'=8] {'bond'}, use_global_device_ids=true, to_apply=%region_3.3 | all-reduce | flops 256 | bytes 2048 | tf_op jit(solution)/shard_map/while/body/eval_jaxpr/psum | solution.py:18
  75.8 20.4 %collective-permute-done = f32[64,3072]{1,0:T(8,128)S(1)} collective-permute-done((f32[64,3072]{1,0:T(8,128)S(1)}, f32[64,3072]{1,0:T(8,128)S(1)}, u32[]{:S(2)}, u32[]{:S(2)}) %collective-permute-start) | collective-permute-done | bytes 786464 | tf_op jit(solution)/shard_map/while/body/eval_jaxpr/ppermute | solution.py:12
  96.4 14.6 %fusion.17 = f32[64,1536]{1,0:T(8,128)S(1)} fusion(f32[3072,1536]{1,0:T(8,128)} %get-tuple-element.314, f32[64,3072]{1,0:T(8,128)S(1)} %get-tuple-element.293, f32[128,3072]{1,0:T(8,128)S(1)} %get-tuple-element.313, s32[]{:T(128)S(6)} %select_n.103, pred[]{:T(512)} %get-tuple-element.312), kind=kOutput, calls=%fused_computation.clone.1 | convolution fusion | flops 3624075264 | bytes 20840452 | tf_op jit(solution)/shard_map/while/body/eval_jaxpr/dot_general | solution.py:52
  111.6 23.6 %psum.13 = f32[64,4]{1,0:T(8,128)S(1)} all-reduce(f32[64,4]{1,0:T(8,128)S(1)} %get-tuple-element.271), channel_id=1, replica_groups=mesh['section'=16,'bond'=8] {'bond'}, use_global_device_ids=true, to_apply=%region_3.3 | all-reduce | flops 256 | bytes 2048 | tf_op jit(solution)/shard_map/while/body/eval_jaxpr/psum | solution.py:18
  151.0 21.9 %collective-permute-done = f32[64,3072]{1,0:T(8,128)S(1)} collective-permute-done((f32[64,3072]{1,0:T(8,128)S(1)}, f32[64,3072]{1,0:T(8,128)S(1)}, u32[]{:S(2)}, u32[]{:S(2)}) %collective-permute-start) | collective-permute-done | bytes 786464 | tf_op jit(solution)/shard_map/while/body/eval_jaxpr/ppermute | solution.py:12
  173.0 14.6 %fusion.17 = f32[64,1536]{1,0:T(8,128)S(1)} fusion(f32[3072,1536]{1,0:T(8,128)} %get-tuple-element.314, f32[64,3072]{1,0:T(8,128)S(1)} %get-tuple-element.293, f32[128,3072]{1,0:T(8,128)S(1)} %get-tuple-element.313, s32[]{:T(128)S(6)} %select_n.103, pred[]{:T(512)} %get-tuple-element.312), kind=kOutput, calls=%fused_computation.clone.1 | convolution fusion | flops 3624075264 | bytes 20840452 | tf_op jit(solution)/shard_map/while/body/eval_jaxpr/dot_general | solution.py:52
  188.2 23.6 %psum.13 = f32[64,4]{1,0:T(8,128)S(1)} all-reduce(f32[64,4]{1,0:T(8,128)S(1)} %get-tuple-element.271), channel_id=1, replica_groups=mesh['section'=16,'bond'=8] {'bond'}, use_global_device_ids=true, to_apply=%region_3.3 | all-reduce | flops 256 | bytes 2048 | tf_op jit(solution)/shard_map/while/body/eval_jaxpr/psum | solution.py:18
  227.6 21.9 %collective-permute-done = f32[64,3072]{1,0:T(8,128)S(1)} collective-permute-done((f32[64,3072]{1,0:T(8,128)S(1)}, f32[64,3072]{1,0:T(8,128)S(1)}, u32[]{:S(2)}, u32[]{:S(2)}) %collective-permute-start) | collective-permute-done | bytes 786464 | tf_op jit(solution)/shard_map/while/body/eval_jaxpr/ppermute | solution.py:12
  249.6 14.6 %fusion.17 = f32[64,1536]{1,0:T(8,128)S(1)} fusion(f32[3072,1536]{1,0:T(8,128)} %get-tuple-element.314, f32[64,3072]{1,0:T(8,128)S(1)} %get-tuple-element.293, f32[128,3072]{1,0:T(8,128)S(1)} %get-tuple-element.313, s32[]{:T(128)S(6)} %select_n.103, pred[]{:T(512)} %get-tuple-element.312), kind=kOutput, calls=%fused_computation.clone.1 | convolution fusion | flops 3624075264 | bytes 20840452 | tf_op jit(solution)/shard_map/while/body/eval_jaxpr/dot_general | solution.py:52
  264.8 23.6 %psum.13 = f32[64,4]{1,0:T(8,128)S(1)} all-reduce(f32[64,4]{1,0:T(8,128)S(1)} %get-tuple-element.271), channel_id=1, replica_groups=mesh['section'=16,'bond'=8] {'bond'}, use_global_device_ids=true, to_apply=%region_3.3 | all-reduce | flops 256 | bytes 2048 | tf_op jit(solution)/shard_map/while/body/eval_jaxpr/psum | solution.py:18
  304.2 21.9 %collective-permute-done = f32[64,3072]{1,0:T(8,128)S(1)} collective-permute-done((f32[64,3072]{1,0:T(8,128)S(1)}, f32[64,3072]{1,0:T(8,128)S(1)}, u32[]{:S(2)}, u32[]{:S(2)}) %collective-permute-start) | collective-permute-done | bytes 786464 | tf_op jit(solution)/shard_map/while/body/eval_jaxpr/ppermute | solution.py:12
  326.2 14.6 %fusion.17 = f32[64,1536]{1,0:T(8,128)S(1)} fusion(f32[3072,1536]{1,0:T(8,128)} %get-tuple-element.314, f32[64,3072]{1,0:T(8,128)S(1)} %get-tuple-element.293, f32[128,3072]{1,0:T(8,128)S(1)} %get-tuple-element.313, s32[]{:T(128)S(6)} %select_n.103, pred[]{:T(512)} %get-tuple-element.312), kind=kOutput, calls=%fused_computation.clone.1 | convolution fusion | flops 3624075264 | bytes 20840452 | tf_op jit(solution)/shard_map/while/body/eval_jaxpr/dot_general | solution.py:52
  341.4 23.6 %psum.13 = f32[64,4]{1,0:T(8,128)S(1)} all-reduce(f32[64,4]{1,0:T(8,128)S(1)} %get-tuple-element.271), channel_id=1, replica_groups=mesh['section'=16,'bond'=8] {'bond'}, use_global_device_ids=true, to_apply=%region_3.3 | all-reduce | flops 256 | bytes 2048 | tf_op jit(solution)/shard_map/while/body/eval_jaxpr/psum | solution.py:18
  380.8 21.9 %collective-permute-done = f32[64,3072]{1,0:T(8,128)S(1)} collective-permute-done((f32[64,3072]{1,0:T(8,128)S(1)}, f32[64,3072]{1,0:T(8,128)S(1)}, u32[]{:S(2)}, u32[]{:S(2)}) %collective-permute-start) | collective-permute-done | bytes 786464 | tf_op jit(solution)/shard_map/while/body/eval_jaxpr/ppermute | solution.py:12
  402.8 14.6 %fusion.17 = f32[64,1536]{1,0:T(8,128)S(1)} fusion(f32[3072,1536]{1,0:T(8,128)} %get-tuple-element.314, f32[64,3072]{1,0:T(8,128)S(1)} %get-tuple-element.293, f32[128,3072]{1,0:T(8,128)S(1)} %get-tuple-element.313, s32[]{:T(128)S(6)} %select_n.103, pred[]{:T(512)} %get-tuple-element.312), kind=kOutput, calls=%fused_computation.clone.1 | convolution fusion | flops 3624075264 | bytes 20840452 | tf_op jit(solution)/shard_map/while/body/eval_jaxpr/dot_general | solution.py:52
  418.1 23.6 %psum.13 = f32[64,4]{1,0:T(8,128)S(1)} all-reduce(f32[64,4]{1,0:T(8,128)S(1)} %get-tuple-element.271), channel_id=1, replica_groups=mesh['section'=16,'bond'=8] {'bond'}, use_global_device_ids=true, to_apply=%region_3.3 | all-reduce | flops 256 | bytes 2048 | tf_op jit(solution)/shard_map/while/body/eval_jaxpr/psum | solution.py:18
  457.4 21.9 %collective-permute-done = f32[64,3072]{1,0:T(8,128)S(1)} collective-permute-done((f32[64,3072]{1,0:T(8,128)S(1)}, f32[64,3072]{1,0:T(8,128)S(1)}, u32[]{:S(2)}, u32[]{:S(2)}) %collective-permute-start) | collective-permute-done | bytes 786464 | tf_op jit(solution)/shard_map/while/body/eval_jaxpr/ppermute | solution.py:12
  479.4 14.6 %fusion.17 = f32[64,1536]{1,0:T(8,128)S(1)} fusion(f32[3072,1536]{1,0:T(8,128)} %get-tuple-element.314, f32[64,3072]{1,0:T(8,128)S(1)} %get-tuple-element.293, f32[128,3072]{1,0:T(8,128)S(1)} %get-tuple-element.313, s32[]{:T(128)S(6)} %select_n.103, pred[]{:T(512)} %get-tuple-element.312), kind=kOutput, calls=%fused_computation.clone.1 | convolution fusion | flops 3624075264 | bytes 20840452 | tf_op jit(solution)/shard_map/while/body/eval_jaxpr/dot_general | solution.py:52
  494.7 23.6 %psum.13 = f32[64,4]{1,0:T(8,128)S(1)} all-reduce(f32[64,4]{1,0:T(8,128)S(1)} %get-tuple-element.271), channel_id=1, replica_groups=mesh['section'=16,'bond'=8] {'bond'}, use_global_device_ids=true, to_apply=%region_3.3 | all-reduce | flops 256 | bytes 2048 | tf_op jit(solution)/shard_map/while/body/eval_jaxpr/psum | solution.py:18
  534.0 21.9 %collective-permute-done = f32[64,3072]{1,0:T(8,128)S(1)} collective-permute-done((f32[64,3072]{1,0:T(8,128)S(1)}, f32[64,3072]{1,0:T(8,128)S(1)}, u32[]{:S(2)}, u32[]{:S(2)}) %collective-permute-start) | collective-permute-done | bytes 786464 | tf_op jit(solution)/shard_map/while/body/eval_jaxpr/ppermute | solution.py:12
  556.0 14.6 %fusion.17 = f32[64,1536]{1,0:T(8,128)S(1)} fusion(f32[3072,1536]{1,0:T(8,128)} %get-tuple-element.314, f32[64,3072]{1,0:T(8,128)S(1)} %get-tuple-element.293, f32[128,3072]{1,0:T(8,128)S(1)} %get-tuple-element.313, s32[]{:T(128)S(6)} %select_n.103, pred[]{:T(512)} %get-tuple-element.312), kind=kOutput, calls=%fused_computation.clone.1 | convolution fusion | flops 3624075264 | bytes 20840452 | tf_op jit(solution)/shard_map/while/body/eval_jaxpr/dot_general | solution.py:52
  571.3 23.6 %psum.13 = f32[64,4]{1,0:T(8,128)S(1)} all-reduce(f32[64,4]{1,0:T(8,128)S(1)} %get-tuple-element.271), channel_id=1, replica_groups=mesh['section'=16,'bond'=8] {'bond'}, use_global_device_ids=true, to_apply=%region_3.3 | all-reduce | flops 256 | bytes 2048 | tf_op jit(solution)/shard_map/while/body/eval_jaxpr/psum | solution.py:18
  610.6 21.9 %collective-permute-done = f32[64,3072]{1,0:T(8,128)S(1)} collective-permute-done((f32[64,3072]{1,0:T(8,128)S(1)}, f32[64,3072]{1,0:T(8,128)S(1)}, u32[]{:S(2)}, u32[]{:S(2)}) %collective-permute-start) | collective-permute-done | bytes 786464 | tf_op jit(solution)/shard_map/while/body/eval_jaxpr/ppermute | solution.py:12
  632.7 14.6 %fusion.17 = f32[64,1536]{1,0:T(8,128)S(1)} fusion(f32[3072,1536]{1,0:T(8,128)} %get-tuple-element.314, f32[64,3072]{1,0:T(8,128)S(1)} %get-tuple-element.293, f32[128,3072]{1,0:T(8,128)S(1)} %get-tuple-element.313, s32[]{:T(128)S(6)} %select_n.103, pred[]{:T(512)} %get-tuple-element.312), kind=kOutput, calls=%fused_computation.clone.1 | convolution fusion | flops 3624075264 | bytes 20840452 | tf_op jit(solution)/shard_map/while/body/eval_jaxpr/dot_general | solution.py:52
  647.9 23.6 %psum.13 = f32[64,4]{1,0:T(8,128)S(1)} all-reduce(f32[64,4]{1,0:T(8,128)S(1)} %get-tuple-element.271), channel_id=1, replica_groups=mesh['section'=16,'bond'=8] {'bond'}, use_global_device_ids=true, to_apply=%region_3.3 | all-reduce | flops 256 | bytes 2048 | tf_op jit(solution)/shard_map/while/body/eval_jaxpr/psum | solution.py:18
  687.3 21.9 %collective-permute-done = f32[64,3072]{1,0:T(8,128)S(1)} collective-permute-done((f32[64,3072]{1,0:T(8,128)S(1)}, f32[64,3072]{1,0:T(8,128)S(1)}, u32[]{:S(2)}, u32[]{:S(2)}) %collective-permute-start) | collective-permute-done | bytes 786464 | tf_op jit(solution)/shard_map/while/body/eval_jaxpr/ppermute | solution.py:12
  709.3 14.6 %fusion.17 = f32[64,1536]{1,0:T(8,128)S(1)} fusion(f32[3072,1536]{1,0:T(8,128)} %get-tuple-element.314, f32[64,3072]{1,0:T(8,128)S(1)} %get-tuple-element.293, f32[128,3072]{1,0:T(8,128)S(1)} %get-tuple-element.313, s32[]{:T(128)S(6)} %select_n.103, pred[]{:T(512)} %get-tuple-element.312), kind=kOutput, calls=%fused_computation.clone.1 | convolution fusion | flops 3624075264 | bytes 20840452 | tf_op jit(solution)/shard_map/while/body/eval_jaxpr/dot_general | solution.py:52
  724.5 23.6 %psum.13 = f32[64,4]{1,0:T(8,128)S(1)} all-reduce(f32[64,4]{1,0:T(8,128)S(1)} %get-tuple-element.271), channel_id=1, replica_groups=mesh['section'=16,'bond'=8] {'bond'}, use_global_device_ids=true, to_apply=%region_3.3 | all-reduce | flops 256 | bytes 2048 | tf_op jit(solution)/shard_map/while/body/eval_jaxpr/psum | solution.py:18
  763.9 21.9 %collective-permute-done = f32[64,3072]{1,0:T(8,128)S(1)} collective-permute-done((f32[64,3072]{1,0:T(8,128)S(1)}, f32[64,3072]{1,0:T(8,128)S(1)}, u32[]{:S(2)}, u32[]{:S(2)}) %collective-permute-start) | collective-permute-done | bytes 786464 | tf_op jit(solution)/shard_map/while/body/eval_jaxpr/ppermute | solution.py:12
  785.9 14.6 %fusion.17 = f32[64,1536]{1,0:T(8,128)S(1)} fusion(f32[3072,1536]{1,0:T(8,128)} %get-tuple-element.314, f32[64,3072]{1,0:T(8,128)S(1)} %get-tuple-element.293, f32[128,3072]{1,0:T(8,128)S(1)} %get-tuple-element.313, s32[]{:T(128)S(6)} %select_n.103, pred[]{:T(512)} %get-tuple-element.312), kind=kOutput, calls=%fused_computation.clone.1 | convolution fusion | flops 3624075264 | bytes 20840452 | tf_op jit(solution)/shard_map/while/body/eval_jaxpr/dot_general | solution.py:52
  801.1 23.6 %psum.13 = f32[64,4]{1,0:T(8,128)S(1)} all-reduce(f32[64,4]{1,0:T(8,128)S(1)} %get-tuple-element.271), channel_id=1, replica_groups=mesh['section'=16,'bond'=8] {'bond'}, use_global_device_ids=true, to_apply=%region_3.3 | all-reduce | flops 256 | bytes 2048 | tf_op jit(solution)/shard_map/while/body/eval_jaxpr/psum | solution.py:18
  840.5 21.9 %collective-permute-done = f32[64,3072]{1,0:T(8,128)S(1)} collective-permute-done((f32[64,3072]{1,0:T(8,128)S(1)}, f32[64,3072]{1,0:T(8,128)S(1)}, u32[]{:S(2)}, u32[]{:S(2)}) %collective-permute-start) | collective-permute-done | bytes 786464 | tf_op jit(solution)/shard_map/while/body/eval_jaxpr/ppermute | solution.py:12
  877.7 23.6 %psum.13 = f32[64,4]{1,0:T(8,128)S(1)} all-reduce(f32[64,4]{1,0:T(8,128)S(1)} %get-tuple-element.271), channel_id=1, replica_groups=mesh['section'=16,'bond'=8] {'bond'}, use_global_device_ids=true, to_apply=%region_3.3 | all-reduce | flops 256 | bytes 2048 | tf_op jit(solution)/shard_map/while/body/eval_jaxpr/psum | solution.py:18
  917.1 21.9 %collective-permute-done = f32[64,3072]{1,0:T(8,128)S(1)} collective-permute-done((f32[64,3072]{1,0:T(8,128)S(1)}, f32[64,3072]{1,0:T(8,128)S(1)}, u32[]{:S(2)}, u32[]{:S(2)}) %collective-permute-start) | collective-permute-done | bytes 786464 | tf_op jit(solution)/shard_map/while/body/eval_jaxpr/ppermute | solution.py:12
  954.4 23.6 %psum.13 = f32[64,4]{1,0:T(8,128)S(1)} all-reduce(f32[64,4]{1,0:T(8,128)S(1)} %get-tuple-element.271), channel_id=1, replica_groups=mesh['section'=16,'bond'=8] {'bond'}, use_global_device_ids=true, to_apply=%region_3.3 | all-reduce | flops 256 | bytes 2048 | tf_op jit(solution)/shard_map/while/body/eval_jaxpr/psum | solution.py:18
  993.7 21.9 %collective-permute-done = f32[64,3072]{1,0:T(8,128)S(1)} collective-permute-done((f32[64,3072]{1,0:T(8,128)S(1)}, f32[64,3072]{1,0:T(8,128)S(1)}, u32[]{:S(2)}, u32[]{:S(2)}) %collective-permute-start) | collective-permute-done | bytes 786464 | tf_op jit(solution)/shard_map/while/body/eval_jaxpr/ppermute | solution.py:12
  1031.0 23.6 %psum.13 = f32[64,4]{1,0:T(8,128)S(1)} all-reduce(f32[64,4]{1,0:T(8,128)S(1)} %get-tuple-element.271), channel_id=1, replica_groups=mesh['section'=16,'bond'=8] {'bond'}, use_global_device_ids=true, to_apply=%region_3.3 | all-reduce | flops 256 | bytes 2048 | tf_op jit(solution)/shard_map/while/body/eval_jaxpr/psum | solution.py:18
  1070.3 21.9 %collective-permute-done = f32[64,3072]{1,0:T(8,128)S(1)} collective-permute-done((f32[64,3072]{1,0:T(8,128)S(1)}, f32[64,3072]{1,0:T(8,128)S(1)}, u32[]{:S(2)}, u32[]{:S(2)}) %collective-permute-start) | collective-permute-done | bytes 786464 | tf_op jit(solution)/shard_map/while/body/eval_jaxpr/ppermute | solution.py:12
  1107.6 23.6 %psum.13 = f32[64,4]{1,0:T(8,128)S(1)} all-reduce(f32[64,4]{1,0:T(8,128)S(1)} %get-tuple-element.271), channel_id=1, replica_groups=mesh['section'=16,'bond'=8] {'bond'}, use_global_device_ids=true, to_apply=%region_3.3 | all-reduce | flops 256 | bytes 2048 | tf_op jit(solution)/shard_map/while/body/eval_jaxpr/psum | solution.py:18
  1146.9 21.9 %collective-permute-done = f32[64,3072]{1,0:T(8,128)S(1)} collective-permute-done((f32[64,3072]{1,0:T(8,128)S(1)}, f32[64,3072]{1,0:T(8,128)S(1)}, u32[]{:S(2)}, u32[]{:S(2)}) %collective-permute-start) | collective-permute-done | bytes 786464 | tf_op jit(solution)/shard_map/while/body/eval_jaxpr/ppermute | solution.py:12
  1169.0 14.6 %fusion.17 = f32[64,1536]{1,0:T(8,128)S(1)} fusion(f32[3072,1536]{1,0:T(8,128)} %get-tuple-element.314, f32[64,3072]{1,0:T(8,128)S(1)} %get-tuple-element.293, f32[128,3072]{1,0:T(8,128)S(1)} %get-tuple-element.313, s32[]{:T(128)S(6)} %select_n.103, pred[]{:T(512)} %get-tuple-element.312), kind=kOutput, calls=%fused_computation.clone.1 | convolution fusion | flops 3624075264 | bytes 20840452 | tf_op jit(solution)/shard_map/while/body/eval_jaxpr/dot_general | solution.py:52
  1184.2 23.6 %psum.13 = f32[64,4]{1,0:T(8,128)S(1)} all-reduce(f32[64,4]{1,0:T(8,128)S(1)} %get-tuple-element.271), channel_id=1, replica_groups=mesh['section'=16,'bond'=8] {'bond'}, use_global_device_ids=true, to_apply=%region_3.3 | all-reduce | flops 256 | bytes 2048 | tf_op jit(solution)/shard_map/while/body/eval_jaxpr/psum | solution.py:18
  1223.6 21.9 %collective-permute-done = f32[64,3072]{1,0:T(8,128)S(1)} collective-permute-done((f32[64,3072]{1,0:T(8,128)S(1)}, f32[64,3072]{1,0:T(8,128)S(1)}, u32[]{:S(2)}, u32[]{:S(2)}) %collective-permute-start) | collective-permute-done | bytes 786464 | tf_op jit(solution)/shard_map/while/body/eval_jaxpr/ppermute | solution.py:12
  1245.6 14.6 %fusion.17 = f32[64,1536]{1,0:T(8,128)S(1)} fusion(f32[3072,1536]{1,0:T(8,128)} %get-tuple-element.314, f32[64,3072]{1,0:T(8,128)S(1)} %get-tuple-element.293, f32[128,3072]{1,0:T(8,128)S(1)} %get-tuple-element.313, s32[]{:T(128)S(6)} %select_n.103, pred[]{:T(512)} %get-tuple-element.312), kind=kOutput, calls=%fused_computation.clone.1 | convolution fusion | flops 3624075264 | bytes 20840452 | tf_op jit(solution)/shard_map/while/body/eval_jaxpr/dot_general | solution.py:52
  1260.8 23.6 %psum.13 = f32[64,4]{1,0:T(8,128)S(1)} all-reduce(f32[64,4]{1,0:T(8,128)S(1)} %get-tuple-element.271), channel_id=1, replica_groups=mesh['section'=16,'bond'=8] {'bond'}, use_global_device_ids=true, to_apply=%region_3.3 | all-reduce | flops 256 | bytes 2048 | tf_op jit(solution)/shard_map/while/body/eval_jaxpr/psum | solution.py:18
  1300.2 21.9 %collective-permute-done = f32[64,3072]{1,0:T(8,128)S(1)} collective-permute-done((f32[64,3072]{1,0:T(8,128)S(1)}, f32[64,3072]{1,0:T(8,128)S(1)}, u32[]{:S(2)}, u32[]{:S(2)}) %collective-permute-start) | collective-permute-done | bytes 786464 | tf_op jit(solution)/shard_map/while/body/eval_jaxpr/ppermute | solution.py:12
  (169 shorter events, 355.4 us)
Async XLA Ops:
  0.6 16.6 %copy-start = (f32[128,3072]{1,0:T(8,128)S(1)}, f32[128,3072]{1,0:T(8,128)}, u32[]{:S(2)}) copy-start(f32[128,3072]{1,0:T(8,128)} %param.6) | copy-start | bytes 4718596
  0.6 16.6 %copy-start.3 = (s32[1,128]{1,0:T(1,128)S(1)}, s32[1,128]{1,0:T(1,128)}, u32[]{:S(2)}) copy-start(s32[1,128]{1,0:T(1,128)} %param.7) | copy-start | bytes 1540
  72.4 23.8 %collective-permute-start = (f32[64,3072]{1,0:T(8,128)S(1)}, f32[64,3072]{1,0:T(8,128)S(1)}, u32[]{:S(2)}, u32[]{:S(2)}) collective-permute-start(f32[64,3072]{1,0:T(8,128)S(1)} %all_gather.9), channel_id=1, source_target_pairs={{0,8},{8,16},{16,24},{24,32},{32,40},{40,48},{48,56},{56,64},{64,7... | collective-permute-start | bytes 2359304 | tf_op jit(solution)/shard_map/while/body/eval_jaxpr/ppermute | solution.py:12
  149.0 23.8 %collective-permute-start = (f32[64,3072]{1,0:T(8,128)S(1)}, f32[64,3072]{1,0:T(8,128)S(1)}, u32[]{:S(2)}, u32[]{:S(2)}) collective-permute-start(f32[64,3072]{1,0:T(8,128)S(1)} %all_gather.9), channel_id=1, source_target_pairs={{0,8},{8,16},{16,24},{24,32},{32,40},{40,48},{48,56},{56,64},{64,7... | collective-permute-start | bytes 2359304 | tf_op jit(solution)/shard_map/while/body/eval_jaxpr/ppermute | solution.py:12
  225.7 23.8 %collective-permute-start = (f32[64,3072]{1,0:T(8,128)S(1)}, f32[64,3072]{1,0:T(8,128)S(1)}, u32[]{:S(2)}, u32[]{:S(2)}) collective-permute-start(f32[64,3072]{1,0:T(8,128)S(1)} %all_gather.9), channel_id=1, source_target_pairs={{0,8},{8,16},{16,24},{24,32},{32,40},{40,48},{48,56},{56,64},{64,7... | collective-permute-start | bytes 2359304 | tf_op jit(solution)/shard_map/while/body/eval_jaxpr/ppermute | solution.py:12
  302.3 23.8 %collective-permute-start = (f32[64,3072]{1,0:T(8,128)S(1)}, f32[64,3072]{1,0:T(8,128)S(1)}, u32[]{:S(2)}, u32[]{:S(2)}) collective-permute-start(f32[64,3072]{1,0:T(8,128)S(1)} %all_gather.9), channel_id=1, source_target_pairs={{0,8},{8,16},{16,24},{24,32},{32,40},{40,48},{48,56},{56,64},{64,7... | collective-permute-start | bytes 2359304 | tf_op jit(solution)/shard_map/while/body/eval_jaxpr/ppermute | solution.py:12
  378.9 23.8 %collective-permute-start = (f32[64,3072]{1,0:T(8,128)S(1)}, f32[64,3072]{1,0:T(8,128)S(1)}, u32[]{:S(2)}, u32[]{:S(2)}) collective-permute-start(f32[64,3072]{1,0:T(8,128)S(1)} %all_gather.9), channel_id=1, source_target_pairs={{0,8},{8,16},{16,24},{24,32},{32,40},{40,48},{48,56},{56,64},{64,7... | collective-permute-start | bytes 2359304 | tf_op jit(solution)/shard_map/while/body/eval_jaxpr/ppermute | solution.py:12
  455.5 23.8 %collective-permute-start = (f32[64,3072]{1,0:T(8,128)S(1)}, f32[64,3072]{1,0:T(8,128)S(1)}, u32[]{:S(2)}, u32[]{:S(2)}) collective-permute-start(f32[64,3072]{1,0:T(8,128)S(1)} %all_gather.9), channel_id=1, source_target_pairs={{0,8},{8,16},{16,24},{24,32},{32,40},{40,48},{48,56},{56,64},{64,7... | collective-permute-start | bytes 2359304 | tf_op jit(solution)/shard_map/while/body/eval_jaxpr/ppermute | solution.py:12
  532.1 23.8 %collective-permute-start = (f32[64,3072]{1,0:T(8,128)S(1)}, f32[64,3072]{1,0:T(8,128)S(1)}, u32[]{:S(2)}, u32[]{:S(2)}) collective-permute-start(f32[64,3072]{1,0:T(8,128)S(1)} %all_gather.9), channel_id=1, source_target_pairs={{0,8},{8,16},{16,24},{24,32},{32,40},{40,48},{48,56},{56,64},{64,7... | collective-permute-start | bytes 2359304 | tf_op jit(solution)/shard_map/while/body/eval_jaxpr/ppermute | solution.py:12
  608.7 23.8 %collective-permute-start = (f32[64,3072]{1,0:T(8,128)S(1)}, f32[64,3072]{1,0:T(8,128)S(1)}, u32[]{:S(2)}, u32[]{:S(2)}) collective-permute-start(f32[64,3072]{1,0:T(8,128)S(1)} %all_gather.9), channel_id=1, source_target_pairs={{0,8},{8,16},{16,24},{24,32},{32,40},{40,48},{48,56},{56,64},{64,7... | collective-permute-start | bytes 2359304 | tf_op jit(solution)/shard_map/while/body/eval_jaxpr/ppermute | solution.py:12
  685.3 23.8 %collective-permute-start = (f32[64,3072]{1,0:T(8,128)S(1)}, f32[64,3072]{1,0:T(8,128)S(1)}, u32[]{:S(2)}, u32[]{:S(2)}) collective-permute-start(f32[64,3072]{1,0:T(8,128)S(1)} %all_gather.9), channel_id=1, source_target_pairs={{0,8},{8,16},{16,24},{24,32},{32,40},{40,48},{48,56},{56,64},{64,7... | collective-permute-start | bytes 2359304 | tf_op jit(solution)/shard_map/while/body/eval_jaxpr/ppermute | solution.py:12
  762.0 23.8 %collective-permute-start = (f32[64,3072]{1,0:T(8,128)S(1)}, f32[64,3072]{1,0:T(8,128)S(1)}, u32[]{:S(2)}, u32[]{:S(2)}) collective-permute-start(f32[64,3072]{1,0:T(8,128)S(1)} %all_gather.9), channel_id=1, source_target_pairs={{0,8},{8,16},{16,24},{24,32},{32,40},{40,48},{48,56},{56,64},{64,7... | collective-permute-start | bytes 2359304 | tf_op jit(solution)/shard_map/while/body/eval_jaxpr/ppermute | solution.py:12
  838.6 23.8 %collective-permute-start = (f32[64,3072]{1,0:T(8,128)S(1)}, f32[64,3072]{1,0:T(8,128)S(1)}, u32[]{:S(2)}, u32[]{:S(2)}) collective-permute-start(f32[64,3072]{1,0:T(8,128)S(1)} %all_gather.9), channel_id=1, source_target_pairs={{0,8},{8,16},{16,24},{24,32},{32,40},{40,48},{48,56},{56,64},{64,7... | collective-permute-start | bytes 2359304 | tf_op jit(solution)/shard_map/while/body/eval_jaxpr/ppermute | solution.py:12
  915.2 23.8 %collective-permute-start = (f32[64,3072]{1,0:T(8,128)S(1)}, f32[64,3072]{1,0:T(8,128)S(1)}, u32[]{:S(2)}, u32[]{:S(2)}) collective-permute-start(f32[64,3072]{1,0:T(8,128)S(1)} %all_gather.9), channel_id=1, source_target_pairs={{0,8},{8,16},{16,24},{24,32},{32,40},{40,48},{48,56},{56,64},{64,7... | collective-permute-start | bytes 2359304 | tf_op jit(solution)/shard_map/while/body/eval_jaxpr/ppermute | solution.py:12
  991.8 23.8 %collective-permute-start = (f32[64,3072]{1,0:T(8,128)S(1)}, f32[64,3072]{1,0:T(8,128)S(1)}, u32[]{:S(2)}, u32[]{:S(2)}) collective-permute-start(f32[64,3072]{1,0:T(8,128)S(1)} %all_gather.9), channel_id=1, source_target_pairs={{0,8},{8,16},{16,24},{24,32},{32,40},{40,48},{48,56},{56,64},{64,7... | collective-permute-start | bytes 2359304 | tf_op jit(solution)/shard_map/while/body/eval_jaxpr/ppermute | solution.py:12
  1068.4 23.8 %collective-permute-start = (f32[64,3072]{1,0:T(8,128)S(1)}, f32[64,3072]{1,0:T(8,128)S(1)}, u32[]{:S(2)}, u32[]{:S(2)}) collective-permute-start(f32[64,3072]{1,0:T(8,128)S(1)} %all_gather.9), channel_id=1, source_target_pairs={{0,8},{8,16},{16,24},{24,32},{32,40},{40,48},{48,56},{56,64},{64,7... | collective-permute-start | bytes 2359304 | tf_op jit(solution)/shard_map/while/body/eval_jaxpr/ppermute | solution.py:12
  1145.0 23.8 %collective-permute-start = (f32[64,3072]{1,0:T(8,128)S(1)}, f32[64,3072]{1,0:T(8,128)S(1)}, u32[]{:S(2)}, u32[]{:S(2)}) collective-permute-start(f32[64,3072]{1,0:T(8,128)S(1)} %all_gather.9), channel_id=1, source_target_pairs={{0,8},{8,16},{16,24},{24,32},{32,40},{40,48},{48,56},{56,64},{64,7... | collective-permute-start | bytes 2359304 | tf_op jit(solution)/shard_map/while/body/eval_jaxpr/ppermute | solution.py:12
  1221.6 23.8 %collective-permute-start = (f32[64,3072]{1,0:T(8,128)S(1)}, f32[64,3072]{1,0:T(8,128)S(1)}, u32[]{:S(2)}, u32[]{:S(2)}) collective-permute-start(f32[64,3072]{1,0:T(8,128)S(1)} %all_gather.9), channel_id=1, source_target_pairs={{0,8},{8,16},{16,24},{24,32},{32,40},{40,48},{48,56},{56,64},{64,7... | collective-permute-start | bytes 2359304 | tf_op jit(solution)/shard_map/while/body/eval_jaxpr/ppermute | solution.py:12
  1298.3 23.8 %collective-permute-start = (f32[64,3072]{1,0:T(8,128)S(1)}, f32[64,3072]{1,0:T(8,128)S(1)}, u32[]{:S(2)}, u32[]{:S(2)}) collective-permute-start(f32[64,3072]{1,0:T(8,128)S(1)} %all_gather.9), channel_id=1, source_target_pairs={{0,8},{8,16},{16,24},{24,32},{32,40},{40,48},{48,56},{56,64},{64,7... | collective-permute-start | bytes 2359304 | tf_op jit(solution)/shard_map/while/body/eval_jaxpr/ppermute | solution.py:12
  1322.0 0.7 copy-start.1
  1322.0 0.7 copy-start.2
where the time goes:
time: 1320 us
  blocking collectives  631 us (48%)
  waiting for transfers between devices  370 us (28%)
  matrix products  249 us (19%)
  starting transfers between devices  33.9 us (3%)
  local copies, waits for them, and re-layouts  20.8 us (2%)
  other arithmetic  16.1 us (1%)
    psum x17, blocking collectives, finish(): weight = lax.psum(partial_weight, 'bond')  403 us
    ppermute x17, waiting for transfers between devices, from_behind(): return lax.ppermute(array, axis, pairs)  370 us
    dot_general x17, matrix products, advance(): jnp.dot(current, site_matrix, precision=lax.Precision.HIGHEST, preferred_...  249 us
    all_gather x17, blocking collectives, advance(): whole_rows = lax.all_gather(next_block, 'bond', axis=1, tiled=True)  228 us
    ppermute x17, starting transfers between devices, from_behind(): return lax.ppermute(array, axis, pairs)  33.9 us
  transfers between devices with their start and end apart: 17, of which 17 were waited for; matrix products, arithmetic and copies ran while one was open for 0% of the time, Pallas kernels for 0%

commit v1 on v0

--- a/solution.py
+++ b/solution.py
@@ -4,6 +4,7 @@
 from jax.sharding import PartitionSpec as P
 
 BATCH = 64
+register_outputs = lambda mat: jnp.sum(lax.all_gather(mat, axis_name="bond"), axis=0)
 
 
 def from_behind(array, axis, by):
@@ -15,7 +16,7 @@
 def finish(amplitudes, chosen, block_rows, outcomes, columns, width):
     shaped = amplitudes.reshape(block_rows, outcomes, columns)
     partial_weight = jnp.sum(shaped * shaped, axis=2)
-    weight = lax.psum(partial_weight, "bond")
+    weight = register_outputs(partial_weight)
     outcome_ids = jnp.arange(outcomes, dtype=jnp.int32)
     onehot = (chosen[:, None] == outcome_ids[None, :]).astype(jnp.float32)
     chosen_weight = jnp.sum(onehot * weight, axis=1)

time: 1320 us -> 1110 us (0.84)
  blocking collectives: 631 us -> 421 us
    psum x17 -> x0, blocking collectives: 403 us -> none  [finish(): weight = lax.psum(partial_weight, 'bond')]
    all_gather x0 -> x17, blocking collectives: none -> 193 us  [lax.all_gather(mat, axis_name='bond')]
where the time goes in v1:
time: 1110 us
  blocking collectives  421 us (38%)
  waiting for transfers between devices  370 us (33%)
  matrix products  249 us (22%)
  starting transfers between devices  33.9 us (3%)
  local copies, waits for them, and re-layouts  23.7 us (2%)
  other arithmetic  12.8 us (1%)
    ppermute x17, waiting for transfers between devices, from_behind(): return lax.ppermute(array, axis, pairs)  370 us
    dot_general x17, matrix products, advance(): jnp.dot(current, site_matrix, precision=lax.Precision.HIGHEST, preferred_...  249 us
    all_gather x17, blocking collectives, advance(): whole_rows = lax.all_gather(next_block, 'bond', axis=1, tiled=True)  228 us
    all_gather x17, blocking collectives, lax.all_gather(mat, axis_name='bond')  193 us
    ppermute x17, starting transfers between devices, from_behind(): return lax.ppermute(array, axis, pairs)  33.9 us
  transfers between devices with their start and end apart: 17, of which 17 were waited for; matrix products, arithmetic and copies ran while one was open for 0% of the time, Pallas kernels for 0%

profile of v1, /device:TPU:96, one launch (start us, length us, event | category | flops | bytes accessed | tf_op | source)
XLA Modules:
  0.0 1111.4 jit_solution(1509919389795837234)
XLA Ops:
  0.7 16.5 %copy.7 = f32[384,8,4,384]{3,1,2,0:T(8,128)} copy(f32[384,8,4,384]{3,2,1,0:T(4,128)} %bitcast.13) | data formatting | bytes 37748736
  17.3 1093.5 %while.18 = (s32[]{:T(128)}, f32[64,3072]{1,0:T(8,128)S(1)}, f32[128]{0:T(128)S(1)}, f32[128,384]{1,0:T(8,128)S(1)}, s32[]{:T(128)}, /*index=5*/s32[128]{0:T(128...) while((s32[]{:T(128)}, f32[64,3072]{1,0:T(8,128)S(1)}, ...), condition=%wide.region_6.7_spmd, body=%wide.region_0.6_spmd.sunk | while | flops 3624498176 | bytes 26572904 | solution.py:72
  17.5 14.6 %fusion.17 = f32[64,1536]{1,0:T(8,128)S(1)} fusion(f32[3072,1536]{1,0:T(8,128)} %get-tuple-element.314, f32[64,3072]{1,0:T(8,128)S(1)} %get-tuple-element.293, f32[128,3072]{1,0:T(8,128)S(1)} %get-tuple-element.313, s32[]{:T(128)S(6)} %select_n.103, pred[]{:T(512)} %get-tuple-element.312), kind=kOutput, calls=%fused_computation.clone.1 | convolution fusion | flops 3624075264 | bytes 20840452 | tf_op jit(solution)/shard_map/while/body/eval_jaxpr/dot_general | solution.py:53
  62.1 20.4 %collective-permute-done = f32[64,3072]{1,0:T(8,128)S(1)} collective-permute-done((f32[64,3072]{1,0:T(8,128)S(1)}, f32[64,3072]{1,0:T(8,128)S(1)}, u32[]{:S(2)}, u32[]{:S(2)}) %collective-permute-start) | collective-permute-done | bytes 786464 | tf_op jit(solution)/shard_map/while/body/eval_jaxpr/ppermute | solution.py:13
  82.6 14.6 %fusion.17 = f32[64,1536]{1,0:T(8,128)S(1)} fusion(f32[3072,1536]{1,0:T(8,128)} %get-tuple-element.314, f32[64,3072]{1,0:T(8,128)S(1)} %get-tuple-element.293, f32[128,3072]{1,0:T(8,128)S(1)} %get-tuple-element.313, s32[]{:T(128)S(6)} %select_n.103, pred[]{:T(512)} %get-tuple-element.312), kind=kOutput, calls=%fused_computation.clone.1 | convolution fusion | flops 3624075264 | bytes 20840452 | tf_op jit(solution)/shard_map/while/body/eval_jaxpr/dot_general | solution.py:53
  124.8 21.9 %collective-permute-done = f32[64,3072]{1,0:T(8,128)S(1)} collective-permute-done((f32[64,3072]{1,0:T(8,128)S(1)}, f32[64,3072]{1,0:T(8,128)S(1)}, u32[]{:S(2)}, u32[]{:S(2)}) %collective-permute-start) | collective-permute-done | bytes 786464 | tf_op jit(solution)/shard_map/while/body/eval_jaxpr/ppermute | solution.py:13
  146.9 14.6 %fusion.17 = f32[64,1536]{1,0:T(8,128)S(1)} fusion(f32[3072,1536]{1,0:T(8,128)} %get-tuple-element.314, f32[64,3072]{1,0:T(8,128)S(1)} %get-tuple-element.293, f32[128,3072]{1,0:T(8,128)S(1)} %get-tuple-element.313, s32[]{:T(128)S(6)} %select_n.103, pred[]{:T(512)} %get-tuple-element.312), kind=kOutput, calls=%fused_computation.clone.1 | convolution fusion | flops 3624075264 | bytes 20840452 | tf_op jit(solution)/shard_map/while/body/eval_jaxpr/dot_general | solution.py:53
  189.1 21.9 %collective-permute-done = f32[64,3072]{1,0:T(8,128)S(1)} collective-permute-done((f32[64,3072]{1,0:T(8,128)S(1)}, f32[64,3072]{1,0:T(8,128)S(1)}, u32[]{:S(2)}, u32[]{:S(2)}) %collective-permute-start) | collective-permute-done | bytes 786464 | tf_op jit(solution)/shard_map/while/body/eval_jaxpr/ppermute | solution.py:13
  211.1 14.6 %fusion.17 = f32[64,1536]{1,0:T(8,128)S(1)} fusion(f32[3072,1536]{1,0:T(8,128)} %get-tuple-element.314, f32[64,3072]{1,0:T(8,128)S(1)} %get-tuple-element.293, f32[128,3072]{1,0:T(8,128)S(1)} %get-tuple-element.313, s32[]{:T(128)S(6)} %select_n.103, pred[]{:T(512)} %get-tuple-element.312), kind=kOutput, calls=%fused_computation.clone.1 | convolution fusion | flops 3624075264 | bytes 20840452 | tf_op jit(solution)/shard_map/while/body/eval_jaxpr/dot_general | solution.py:53
  238.0 13.4 %all_gather.25 = f32[64,3072]{1,0:T(8,128)S(1)} all-gather(f32[64,384]{1,0:T(8,128)S(1)} %get-tuple-element.275), channel_id=1, replica_groups=mesh['section'=16,'bond'=8] {'bond'}, dimensions={1}, use_global_device_ids=true | all-gather | bytes 884736 | tf_op jit(solution)/shard_map/while/body/eval_jaxpr/all_gather | solution.py:68
  253.4 21.9 %collective-permute-done = f32[64,3072]{1,0:T(8,128)S(1)} collective-permute-done((f32[64,3072]{1,0:T(8,128)S(1)}, f32[64,3072]{1,0:T(8,128)S(1)}, u32[]{:S(2)}, u32[]{:S(2)}) %collective-permute-start) | collective-permute-done | bytes 786464 | tf_op jit(solution)/shard_map/while/body/eval_jaxpr/ppermute | solution.py:13
  275.4 14.6 %fusion.17 = f32[64,1536]{1,0:T(8,128)S(1)} fusion(f32[3072,1536]{1,0:T(8,128)} %get-tuple-element.314, f32[64,3072]{1,0:T(8,128)S(1)} %get-tuple-element.293, f32[128,3072]{1,0:T(8,128)S(1)} %get-tuple-element.313, s32[]{:T(128)S(6)} %select_n.103, pred[]{:T(512)} %get-tuple-element.312), kind=kOutput, calls=%fused_computation.clone.1 | convolution fusion | flops 3624075264 | bytes 20840452 | tf_op jit(solution)/shard_map/while/body/eval_jaxpr/dot_general | solution.py:53
  302.3 13.4 %all_gather.25 = f32[64,3072]{1,0:T(8,128)S(1)} all-gather(f32[64,384]{1,0:T(8,128)S(1)} %get-tuple-element.275), channel_id=1, replica_groups=mesh['section'=16,'bond'=8] {'bond'}, dimensions={1}, use_global_device_ids=true | all-gather | bytes 884736 | tf_op jit(solution)/shard_map/while/body/eval_jaxpr/all_gather | solution.py:68
  317.6 21.9 %collective-permute-done = f32[64,3072]{1,0:T(8,128)S(1)} collective-permute-done((f32[64,3072]{1,0:T(8,128)S(1)}, f32[64,3072]{1,0:T(8,128)S(1)}, u32[]{:S(2)}, u32[]{:S(2)}) %collective-permute-start) | collective-permute-done | bytes 786464 | tf_op jit(solution)/shard_map/while/body/eval_jaxpr/ppermute | solution.py:13
  339.7 14.6 %fusion.17 = f32[64,1536]{1,0:T(8,128)S(1)} fusion(f32[3072,1536]{1,0:T(8,128)} %get-tuple-element.314, f32[64,3072]{1,0:T(8,128)S(1)} %get-tuple-element.293, f32[128,3072]{1,0:T(8,128)S(1)} %get-tuple-element.313, s32[]{:T(128)S(6)} %select_n.103, pred[]{:T(512)} %get-tuple-element.312), kind=kOutput, calls=%fused_computation.clone.1 | convolution fusion | flops 3624075264 | bytes 20840452 | tf_op jit(solution)/shard_map/while/body/eval_jaxpr/dot_general | solution.py:53
  366.6 13.4 %all_gather.25 = f32[64,3072]{1,0:T(8,128)S(1)} all-gather(f32[64,384]{1,0:T(8,128)S(1)} %get-tuple-element.275), channel_id=1, replica_groups=mesh['section'=16,'bond'=8] {'bond'}, dimensions={1}, use_global_device_ids=true | all-gather | bytes 884736 | tf_op jit(solution)/shard_map/while/body/eval_jaxpr/all_gather | solution.py:68
  381.9 21.9 %collective-permute-done = f32[64,3072]{1,0:T(8,128)S(1)} collective-permute-done((f32[64,3072]{1,0:T(8,128)S(1)}, f32[64,3072]{1,0:T(8,128)S(1)}, u32[]{:S(2)}, u32[]{:S(2)}) %collective-permute-start) | collective-permute-done | bytes 786464 | tf_op jit(solution)/shard_map/while/body/eval_jaxpr/ppermute | solution.py:13
  403.9 14.6 %fusion.17 = f32[64,1536]{1,0:T(8,128)S(1)} fusion(f32[3072,1536]{1,0:T(8,128)} %get-tuple-element.314, f32[64,3072]{1,0:T(8,128)S(1)} %get-tuple-element.293, f32[128,3072]{1,0:T(8,128)S(1)} %get-tuple-element.313, s32[]{:T(128)S(6)} %select_n.103, pred[]{:T(512)} %get-tuple-element.312), kind=kOutput, calls=%fused_computation.clone.1 | convolution fusion | flops 3624075264 | bytes 20840452 | tf_op jit(solution)/shard_map/while/body/eval_jaxpr/dot_general | solution.py:53
  446.2 21.9 %collective-permute-done = f32[64,3072]{1,0:T(8,128)S(1)} collective-permute-done((f32[64,3072]{1,0:T(8,128)S(1)}, f32[64,3072]{1,0:T(8,128)S(1)}, u32[]{:S(2)}, u32[]{:S(2)}) %collective-permute-start) | collective-permute-done | bytes 786464 | tf_op jit(solution)/shard_map/while/body/eval_jaxpr/ppermute | solution.py:13
  468.2 14.6 %fusion.17 = f32[64,1536]{1,0:T(8,128)S(1)} fusion(f32[3072,1536]{1,0:T(8,128)} %get-tuple-element.314, f32[64,3072]{1,0:T(8,128)S(1)} %get-tuple-element.293, f32[128,3072]{1,0:T(8,128)S(1)} %get-tuple-element.313, s32[]{:T(128)S(6)} %select_n.103, pred[]{:T(512)} %get-tuple-element.312), kind=kOutput, calls=%fused_computation.clone.1 | convolution fusion | flops 3624075264 | bytes 20840452 | tf_op jit(solution)/shard_map/while/body/eval_jaxpr/dot_general | solution.py:53
  495.1 13.4 %all_gather.25 = f32[64,3072]{1,0:T(8,128)S(1)} all-gather(f32[64,384]{1,0:T(8,128)S(1)} %get-tuple-element.275), channel_id=1, replica_groups=mesh['section'=16,'bond'=8] {'bond'}, dimensions={1}, use_global_device_ids=true | all-gather | bytes 884736 | tf_op jit(solution)/shard_map/while/body/eval_jaxpr/all_gather | solution.py:68
  510.4 21.9 %collective-permute-done = f32[64,3072]{1,0:T(8,128)S(1)} collective-permute-done((f32[64,3072]{1,0:T(8,128)S(1)}, f32[64,3072]{1,0:T(8,128)S(1)}, u32[]{:S(2)}, u32[]{:S(2)}) %collective-permute-start) | collective-permute-done | bytes 786464 | tf_op jit(solution)/shard_map/while/body/eval_jaxpr/ppermute | solution.py:13
  532.5 14.6 %fusion.17 = f32[64,1536]{1,0:T(8,128)S(1)} fusion(f32[3072,1536]{1,0:T(8,128)} %get-tuple-element.314, f32[64,3072]{1,0:T(8,128)S(1)} %get-tuple-element.293, f32[128,3072]{1,0:T(8,128)S(1)} %get-tuple-element.313, s32[]{:T(128)S(6)} %select_n.103, pred[]{:T(512)} %get-tuple-element.312), kind=kOutput, calls=%fused_computation.clone.1 | convolution fusion | flops 3624075264 | bytes 20840452 | tf_op jit(solution)/shard_map/while/body/eval_jaxpr/dot_general | solution.py:53
  559.4 13.4 %all_gather.25 = f32[64,3072]{1,0:T(8,128)S(1)} all-gather(f32[64,384]{1,0:T(8,128)S(1)} %get-tuple-element.275), channel_id=1, replica_groups=mesh['section'=16,'bond'=8] {'bond'}, dimensions={1}, use_global_device_ids=true | all-gather | bytes 884736 | tf_op jit(solution)/shard_map/while/body/eval_jaxpr/all_gather | solution.py:68
  574.7 21.9 %collective-permute-done = f32[64,3072]{1,0:T(8,128)S(1)} collective-permute-done((f32[64,3072]{1,0:T(8,128)S(1)}, f32[64,3072]{1,0:T(8,128)S(1)}, u32[]{:S(2)}, u32[]{:S(2)}) %collective-permute-start) | collective-permute-done | bytes 786464 | tf_op jit(solution)/shard_map/while/body/eval_jaxpr/ppermute | solution.py:13
  596.8 14.6 %fusion.17 = f32[64,1536]{1,0:T(8,128)S(1)} fusion(f32[3072,1536]{1,0:T(8,128)} %get-tuple-element.314, f32[64,3072]{1,0:T(8,128)S(1)} %get-tuple-element.293, f32[128,3072]{1,0:T(8,128)S(1)} %get-tuple-element.313, s32[]{:T(128)S(6)} %select_n.103, pred[]{:T(512)} %get-tuple-element.312), kind=kOutput, calls=%fused_computation.clone.1 | convolution fusion | flops 3624075264 | bytes 20840452 | tf_op jit(solution)/shard_map/while/body/eval_jaxpr/dot_general | solution.py:53
  639.0 21.9 %collective-permute-done = f32[64,3072]{1,0:T(8,128)S(1)} collective-permute-done((f32[64,3072]{1,0:T(8,128)S(1)}, f32[64,3072]{1,0:T(8,128)S(1)}, u32[]{:S(2)}, u32[]{:S(2)}) %collective-permute-start) | collective-permute-done | bytes 786464 | tf_op jit(solution)/shard_map/while/body/eval_jaxpr/ppermute | solution.py:13
  661.0 14.6 %fusion.17 = f32[64,1536]{1,0:T(8,128)S(1)} fusion(f32[3072,1536]{1,0:T(8,128)} %get-tuple-element.314, f32[64,3072]{1,0:T(8,128)S(1)} %get-tuple-element.293, f32[128,3072]{1,0:T(8,128)S(1)} %get-tuple-element.313, s32[]{:T(128)S(6)} %select_n.103, pred[]{:T(512)} %get-tuple-element.312), kind=kOutput, calls=%fused_computation.clone.1 | convolution fusion | flops 3624075264 | bytes 20840452 | tf_op jit(solution)/shard_map/while/body/eval_jaxpr/dot_general | solution.py:53
  687.9 13.4 %all_gather.25 = f32[64,3072]{1,0:T(8,128)S(1)} all-gather(f32[64,384]{1,0:T(8,128)S(1)} %get-tuple-element.275), channel_id=1, replica_groups=mesh['section'=16,'bond'=8] {'bond'}, dimensions={1}, use_global_device_ids=true | all-gather | bytes 884736 | tf_op jit(solution)/shard_map/while/body/eval_jaxpr/all_gather | solution.py:68
  703.3 21.9 %collective-permute-done = f32[64,3072]{1,0:T(8,128)S(1)} collective-permute-done((f32[64,3072]{1,0:T(8,128)S(1)}, f32[64,3072]{1,0:T(8,128)S(1)}, u32[]{:S(2)}, u32[]{:S(2)}) %collective-permute-start) | collective-permute-done | bytes 786464 | tf_op jit(solution)/shard_map/while/body/eval_jaxpr/ppermute | solution.py:13
  725.3 14.6 %fusion.17 = f32[64,1536]{1,0:T(8,128)S(1)} fusion(f32[3072,1536]{1,0:T(8,128)} %get-tuple-element.314, f32[64,3072]{1,0:T(8,128)S(1)} %get-tuple-element.293, f32[128,3072]{1,0:T(8,128)S(1)} %get-tuple-element.313, s32[]{:T(128)S(6)} %select_n.103, pred[]{:T(512)} %get-tuple-element.312), kind=kOutput, calls=%fused_computation.clone.1 | convolution fusion | flops 3624075264 | bytes 20840452 | tf_op jit(solution)/shard_map/while/body/eval_jaxpr/dot_general | solution.py:53
  752.2 13.4 %all_gather.25 = f32[64,3072]{1,0:T(8,128)S(1)} all-gather(f32[64,384]{1,0:T(8,128)S(1)} %get-tuple-element.275), channel_id=1, replica_groups=mesh['section'=16,'bond'=8] {'bond'}, dimensions={1}, use_global_device_ids=true | all-gather | bytes 884736 | tf_op jit(solution)/shard_map/while/body/eval_jaxpr/all_gather | solution.py:68
  767.5 21.9 %collective-permute-done = f32[64,3072]{1,0:T(8,128)S(1)} collective-permute-done((f32[64,3072]{1,0:T(8,128)S(1)}, f32[64,3072]{1,0:T(8,128)S(1)}, u32[]{:S(2)}, u32[]{:S(2)}) %collective-permute-start) | collective-permute-done | bytes 786464 | tf_op jit(solution)/shard_map/while/body/eval_jaxpr/ppermute | solution.py:13
  789.6 14.6 %fusion.17 = f32[64,1536]{1,0:T(8,128)S(1)} fusion(f32[3072,1536]{1,0:T(8,128)} %get-tuple-element.314, f32[64,3072]{1,0:T(8,128)S(1)} %get-tuple-element.293, f32[128,3072]{1,0:T(8,128)S(1)} %get-tuple-element.313, s32[]{:T(128)S(6)} %select_n.103, pred[]{:T(512)} %get-tuple-element.312), kind=kOutput, calls=%fused_computation.clone.1 | convolution fusion | flops 3624075264 | bytes 20840452 | tf_op jit(solution)/shard_map/while/body/eval_jaxpr/dot_general | solution.py:53
  816.5 13.4 %all_gather.25 = f32[64,3072]{1,0:T(8,128)S(1)} all-gather(f32[64,384]{1,0:T(8,128)S(1)} %get-tuple-element.275), channel_id=1, replica_groups=mesh['section'=16,'bond'=8] {'bond'}, dimensions={1}, use_global_device_ids=true | all-gather | bytes 884736 | tf_op jit(solution)/shard_map/while/body/eval_jaxpr/all_gather | solution.py:68
  831.8 21.9 %collective-permute-done = f32[64,3072]{1,0:T(8,128)S(1)} collective-permute-done((f32[64,3072]{1,0:T(8,128)S(1)}, f32[64,3072]{1,0:T(8,128)S(1)}, u32[]{:S(2)}, u32[]{:S(2)}) %collective-permute-start) | collective-permute-done | bytes 786464 | tf_op jit(solution)/shard_map/while/body/eval_jaxpr/ppermute | solution.py:13
  853.8 14.6 %fusion.17 = f32[64,1536]{1,0:T(8,128)S(1)} fusion(f32[3072,1536]{1,0:T(8,128)} %get-tuple-element.314, f32[64,3072]{1,0:T(8,128)S(1)} %get-tuple-element.293, f32[128,3072]{1,0:T(8,128)S(1)} %get-tuple-element.313, s32[]{:T(128)S(6)} %select_n.103, pred[]{:T(512)} %get-tuple-element.312), kind=kOutput, calls=%fused_computation.clone.1 | convolution fusion | flops 3624075264 | bytes 20840452 | tf_op jit(solution)/shard_map/while/body/eval_jaxpr/dot_general | solution.py:53
  880.7 13.4 %all_gather.25 = f32[64,3072]{1,0:T(8,128)S(1)} all-gather(f32[64,384]{1,0:T(8,128)S(1)} %get-tuple-element.275), channel_id=1, replica_groups=mesh['section'=16,'bond'=8] {'bond'}, dimensions={1}, use_global_device_ids=true | all-gather | bytes 884736 | tf_op jit(solution)/shard_map/while/body/eval_jaxpr/all_gather | solution.py:68
  896.1 21.9 %collective-permute-done = f32[64,3072]{1,0:T(8,128)S(1)} collective-permute-done((f32[64,3072]{1,0:T(8,128)S(1)}, f32[64,3072]{1,0:T(8,128)S(1)}, u32[]{:S(2)}, u32[]{:S(2)}) %collective-permute-start) | collective-permute-done | bytes 786464 | tf_op jit(solution)/shard_map/while/body/eval_jaxpr/ppermute | solution.py:13
  918.1 14.6 %fusion.17 = f32[64,1536]{1,0:T(8,128)S(1)} fusion(f32[3072,1536]{1,0:T(8,128)} %get-tuple-element.314, f32[64,3072]{1,0:T(8,128)S(1)} %get-tuple-element.293, f32[128,3072]{1,0:T(8,128)S(1)} %get-tuple-element.313, s32[]{:T(128)S(6)} %select_n.103, pred[]{:T(512)} %get-tuple-element.312), kind=kOutput, calls=%fused_computation.clone.1 | convolution fusion | flops 3624075264 | bytes 20840452 | tf_op jit(solution)/shard_map/while/body/eval_jaxpr/dot_general | solution.py:53
  945.0 13.4 %all_gather.25 = f32[64,3072]{1,0:T(8,128)S(1)} all-gather(f32[64,384]{1,0:T(8,128)S(1)} %get-tuple-element.275), channel_id=1, replica_groups=mesh['section'=16,'bond'=8] {'bond'}, dimensions={1}, use_global_device_ids=true | all-gather | bytes 884736 | tf_op jit(solution)/shard_map/while/body/eval_jaxpr/all_gather | solution.py:68
  960.3 21.9 %collective-permute-done = f32[64,3072]{1,0:T(8,128)S(1)} collective-permute-done((f32[64,3072]{1,0:T(8,128)S(1)}, f32[64,3072]{1,0:T(8,128)S(1)}, u32[]{:S(2)}, u32[]{:S(2)}) %collective-permute-start) | collective-permute-done | bytes 786464 | tf_op jit(solution)/shard_map/while/body/eval_jaxpr/ppermute | solution.py:13
  982.4 14.6 %fusion.17 = f32[64,1536]{1,0:T(8,128)S(1)} fusion(f32[3072,1536]{1,0:T(8,128)} %get-tuple-element.314, f32[64,3072]{1,0:T(8,128)S(1)} %get-tuple-element.293, f32[128,3072]{1,0:T(8,128)S(1)} %get-tuple-element.313, s32[]{:T(128)S(6)} %select_n.103, pred[]{:T(512)} %get-tuple-element.312), kind=kOutput, calls=%fused_computation.clone.1 | convolution fusion | flops 3624075264 | bytes 20840452 | tf_op jit(solution)/shard_map/while/body/eval_jaxpr/dot_general | solution.py:53
  1009.3 13.4 %all_gather.25 = f32[64,3072]{1,0:T(8,128)S(1)} all-gather(f32[64,384]{1,0:T(8,128)S(1)} %get-tuple-element.275), channel_id=1, replica_groups=mesh['section'=16,'bond'=8] {'bond'}, dimensions={1}, use_global_device_ids=true | all-gather | bytes 884736 | tf_op jit(solution)/shard_map/while/body/eval_jaxpr/all_gather | solution.py:68
  1024.6 21.9 %collective-permute-done = f32[64,3072]{1,0:T(8,128)S(1)} collective-permute-done((f32[64,3072]{1,0:T(8,128)S(1)}, f32[64,3072]{1,0:T(8,128)S(1)}, u32[]{:S(2)}, u32[]{:S(2)}) %collective-permute-start) | collective-permute-done | bytes 786464 | tf_op jit(solution)/shard_map/while/body/eval_jaxpr/ppermute | solution.py:13
  1046.6 14.6 %fusion.17 = f32[64,1536]{1,0:T(8,128)S(1)} fusion(f32[3072,1536]{1,0:T(8,128)} %get-tuple-element.314, f32[64,3072]{1,0:T(8,128)S(1)} %get-tuple-element.293, f32[128,3072]{1,0:T(8,128)S(1)} %get-tuple-element.313, s32[]{:T(128)S(6)} %select_n.103, pred[]{:T(512)} %get-tuple-element.312), kind=kOutput, calls=%fused_computation.clone.1 | convolution fusion | flops 3624075264 | bytes 20840452 | tf_op jit(solution)/shard_map/while/body/eval_jaxpr/dot_general | solution.py:53
  1073.5 13.4 %all_gather.25 = f32[64,3072]{1,0:T(8,128)S(1)} all-gather(f32[64,384]{1,0:T(8,128)S(1)} %get-tuple-element.275), channel_id=1, replica_groups=mesh['section'=16,'bond'=8] {'bond'}, dimensions={1}, use_global_device_ids=true | all-gather | bytes 884736 | tf_op jit(solution)/shard_map/while/body/eval_jaxpr/all_gather | solution.py:68
  1088.9 21.9 %collective-permute-done = f32[64,3072]{1,0:T(8,128)S(1)} collective-permute-done((f32[64,3072]{1,0:T(8,128)S(1)}, f32[64,3072]{1,0:T(8,128)S(1)}, u32[]{:S(2)}, u32[]{:S(2)}) %collective-permute-start) | collective-permute-done | bytes 786464 | tf_op jit(solution)/shard_map/while/body/eval_jaxpr/ppermute | solution.py:13
  (220 shorter events, 313.7 us)
Async XLA Ops:
  0.6 16.6 %copy-start = (f32[128,3072]{1,0:T(8,128)S(1)}, f32[128,3072]{1,0:T(8,128)}, u32[]{:S(2)}) copy-start(f32[128,3072]{1,0:T(8,128)} %param.6) | copy-start | bytes 4718596
  0.6 16.6 %copy-start.3 = (s32[1,128]{1,0:T(1,128)S(1)}, s32[1,128]{1,0:T(1,128)}, u32[]{:S(2)}) copy-start(s32[1,128]{1,0:T(1,128)} %param.7) | copy-start | bytes 1540
  58.7 23.8 %collective-permute-start = (f32[64,3072]{1,0:T(8,128)S(1)}, f32[64,3072]{1,0:T(8,128)S(1)}, u32[]{:S(2)}, u32[]{:S(2)}) collective-permute-start(f32[64,3072]{1,0:T(8,128)S(1)} %all_gather.25), channel_id=1, source_target_pairs={{0,8},{8,16},{16,24},{24,32},{32,40},{40,48},{48,56},{56,64},{64,7... | collective-permute-start | bytes 2359304 | tf_op jit(solution)/shard_map/while/body/eval_jaxpr/ppermute | solution.py:13
  122.9 23.8 %collective-permute-start = (f32[64,3072]{1,0:T(8,128)S(1)}, f32[64,3072]{1,0:T(8,128)S(1)}, u32[]{:S(2)}, u32[]{:S(2)}) collective-permute-start(f32[64,3072]{1,0:T(8,128)S(1)} %all_gather.25), channel_id=1, source_target_pairs={{0,8},{8,16},{16,24},{24,32},{32,40},{40,48},{48,56},{56,64},{64,7... | collective-permute-start | bytes 2359304 | tf_op jit(solution)/shard_map/while/body/eval_jaxpr/ppermute | solution.py:13
  187.2 23.8 %collective-permute-start = (f32[64,3072]{1,0:T(8,128)S(1)}, f32[64,3072]{1,0:T(8,128)S(1)}, u32[]{:S(2)}, u32[]{:S(2)}) collective-permute-start(f32[64,3072]{1,0:T(8,128)S(1)} %all_gather.25), channel_id=1, source_target_pairs={{0,8},{8,16},{16,24},{24,32},{32,40},{40,48},{48,56},{56,64},{64,7... | collective-permute-start | bytes 2359304 | tf_op jit(solution)/shard_map/while/body/eval_jaxpr/ppermute | solution.py:13
  251.4 23.8 %collective-permute-start = (f32[64,3072]{1,0:T(8,128)S(1)}, f32[64,3072]{1,0:T(8,128)S(1)}, u32[]{:S(2)}, u32[]{:S(2)}) collective-permute-start(f32[64,3072]{1,0:T(8,128)S(1)} %all_gather.25), channel_id=1, source_target_pairs={{0,8},{8,16},{16,24},{24,32},{32,40},{40,48},{48,56},{56,64},{64,7... | collective-permute-start | bytes 2359304 | tf_op jit(solution)/shard_map/while/body/eval_jaxpr/ppermute | solution.py:13
  315.7 23.8 %collective-permute-start = (f32[64,3072]{1,0:T(8,128)S(1)}, f32[64,3072]{1,0:T(8,128)S(1)}, u32[]{:S(2)}, u32[]{:S(2)}) collective-permute-start(f32[64,3072]{1,0:T(8,128)S(1)} %all_gather.25), channel_id=1, source_target_pairs={{0,8},{8,16},{16,24},{24,32},{32,40},{40,48},{48,56},{56,64},{64,7... | collective-permute-start | bytes 2359304 | tf_op jit(solution)/shard_map/while/body/eval_jaxpr/ppermute | solution.py:13
  380.0 23.8 %collective-permute-start = (f32[64,3072]{1,0:T(8,128)S(1)}, f32[64,3072]{1,0:T(8,128)S(1)}, u32[]{:S(2)}, u32[]{:S(2)}) collective-permute-start(f32[64,3072]{1,0:T(8,128)S(1)} %all_gather.25), channel_id=1, source_target_pairs={{0,8},{8,16},{16,24},{24,32},{32,40},{40,48},{48,56},{56,64},{64,7... | collective-permute-start | bytes 2359304 | tf_op jit(solution)/shard_map/while/body/eval_jaxpr/ppermute | solution.py:13
  444.3 23.8 %collective-permute-start = (f32[64,3072]{1,0:T(8,128)S(1)}, f32[64,3072]{1,0:T(8,128)S(1)}, u32[]{:S(2)}, u32[]{:S(2)}) collective-permute-start(f32[64,3072]{1,0:T(8,128)S(1)} %all_gather.25), channel_id=1, source_target_pairs={{0,8},{8,16},{16,24},{24,32},{32,40},{40,48},{48,56},{56,64},{64,7... | collective-permute-start | bytes 2359304 | tf_op jit(solution)/shard_map/while/body/eval_jaxpr/ppermute | solution.py:13
  508.5 23.8 %collective-permute-start = (f32[64,3072]{1,0:T(8,128)S(1)}, f32[64,3072]{1,0:T(8,128)S(1)}, u32[]{:S(2)}, u32[]{:S(2)}) collective-permute-start(f32[64,3072]{1,0:T(8,128)S(1)} %all_gather.25), channel_id=1, source_target_pairs={{0,8},{8,16},{16,24},{24,32},{32,40},{40,48},{48,56},{56,64},{64,7... | collective-permute-start | bytes 2359304 | tf_op jit(solution)/shard_map/while/body/eval_jaxpr/ppermute | solution.py:13
  572.8 23.8 %collective-permute-start = (f32[64,3072]{1,0:T(8,128)S(1)}, f32[64,3072]{1,0:T(8,128)S(1)}, u32[]{:S(2)}, u32[]{:S(2)}) collective-permute-start(f32[64,3072]{1,0:T(8,128)S(1)} %all_gather.25), channel_id=1, source_target_pairs={{0,8},{8,16},{16,24},{24,32},{32,40},{40,48},{48,56},{56,64},{64,7... | collective-permute-start | bytes 2359304 | tf_op jit(solution)/shard_map/while/body/eval_jaxpr/ppermute | solution.py:13
  637.1 23.8 %collective-permute-start = (f32[64,3072]{1,0:T(8,128)S(1)}, f32[64,3072]{1,0:T(8,128)S(1)}, u32[]{:S(2)}, u32[]{:S(2)}) collective-permute-start(f32[64,3072]{1,0:T(8,128)S(1)} %all_gather.25), channel_id=1, source_target_pairs={{0,8},{8,16},{16,24},{24,32},{32,40},{40,48},{48,56},{56,64},{64,7... | collective-permute-start | bytes 2359304 | tf_op jit(solution)/shard_map/while/body/eval_jaxpr/ppermute | solution.py:13
  701.3 23.8 %collective-permute-start = (f32[64,3072]{1,0:T(8,128)S(1)}, f32[64,3072]{1,0:T(8,128)S(1)}, u32[]{:S(2)}, u32[]{:S(2)}) collective-permute-start(f32[64,3072]{1,0:T(8,128)S(1)} %all_gather.25), channel_id=1, source_target_pairs={{0,8},{8,16},{16,24},{24,32},{32,40},{40,48},{48,56},{56,64},{64,7... | collective-permute-start | bytes 2359304 | tf_op jit(solution)/shard_map/while/body/eval_jaxpr/ppermute | solution.py:13
  765.6 23.8 %collective-permute-start = (f32[64,3072]{1,0:T(8,128)S(1)}, f32[64,3072]{1,0:T(8,128)S(1)}, u32[]{:S(2)}, u32[]{:S(2)}) collective-permute-start(f32[64,3072]{1,0:T(8,128)S(1)} %all_gather.25), channel_id=1, source_target_pairs={{0,8},{8,16},{16,24},{24,32},{32,40},{40,48},{48,56},{56,64},{64,7... | collective-permute-start | bytes 2359304 | tf_op jit(solution)/shard_map/while/body/eval_jaxpr/ppermute | solution.py:13
  829.9 23.8 %collective-permute-start = (f32[64,3072]{1,0:T(8,128)S(1)}, f32[64,3072]{1,0:T(8,128)S(1)}, u32[]{:S(2)}, u32[]{:S(2)}) collective-permute-start(f32[64,3072]{1,0:T(8,128)S(1)} %all_gather.25), channel_id=1, source_target_pairs={{0,8},{8,16},{16,24},{24,32},{32,40},{40,48},{48,56},{56,64},{64,7... | collective-permute-start | bytes 2359304 | tf_op jit(solution)/shard_map/while/body/eval_jaxpr/ppermute | solution.py:13
  894.1 23.8 %collective-permute-start = (f32[64,3072]{1,0:T(8,128)S(1)}, f32[64,3072]{1,0:T(8,128)S(1)}, u32[]{:S(2)}, u32[]{:S(2)}) collective-permute-start(f32[64,3072]{1,0:T(8,128)S(1)} %all_gather.25), channel_id=1, source_target_pairs={{0,8},{8,16},{16,24},{24,32},{32,40},{40,48},{48,56},{56,64},{64,7... | collective-permute-start | bytes 2359304 | tf_op jit(solution)/shard_map/while/body/eval_jaxpr/ppermute | solution.py:13
  958.4 23.8 %collective-permute-start = (f32[64,3072]{1,0:T(8,128)S(1)}, f32[64,3072]{1,0:T(8,128)S(1)}, u32[]{:S(2)}, u32[]{:S(2)}) collective-permute-start(f32[64,3072]{1,0:T(8,128)S(1)} %all_gather.25), channel_id=1, source_target_pairs={{0,8},{8,16},{16,24},{24,32},{32,40},{40,48},{48,56},{56,64},{64,7... | collective-permute-start | bytes 2359304 | tf_op jit(solution)/shard_map/while/body/eval_jaxpr/ppermute | solution.py:13
  1022.7 23.8 %collective-permute-start = (f32[64,3072]{1,0:T(8,128)S(1)}, f32[64,3072]{1,0:T(8,128)S(1)}, u32[]{:S(2)}, u32[]{:S(2)}) collective-permute-start(f32[64,3072]{1,0:T(8,128)S(1)} %all_gather.25), channel_id=1, source_target_pairs={{0,8},{8,16},{16,24},{24,32},{32,40},{40,48},{48,56},{56,64},{64,7... | collective-permute-start | bytes 2359304 | tf_op jit(solution)/shard_map/while/body/eval_jaxpr/ppermute | solution.py:13
  1086.9 23.8 %collective-permute-start = (f32[64,3072]{1,0:T(8,128)S(1)}, f32[64,3072]{1,0:T(8,128)S(1)}, u32[]{:S(2)}, u32[]{:S(2)}) collective-permute-start(f32[64,3072]{1,0:T(8,128)S(1)} %all_gather.25), channel_id=1, source_target_pairs={{0,8},{8,16},{16,24},{24,32},{32,40},{40,48},{48,56},{56,64},{64,7... | collective-permute-start | bytes 2359304 | tf_op jit(solution)/shard_map/while/body/eval_jaxpr/ppermute | solution.py:13
  1110.7 0.7 copy-start.1
  1110.7 0.7 copy-start.2
